TPU v7x, 32 devices: a whole 2x2x4 slice. The times are simulated.
32 devices in a mesh: row: 2 (over x), col: 16 (over z, y, core).
Axes of the slice: x: 2, y: 2, z: 4, core: 2. Of those that a mesh axis runs over, the one named last changes fastest.
Arguments:
- factors: bfloat16 [96, 256, 1024], P('col'), may hold values from -0.796875 to 0.796875
- metric_root: bfloat16 [1024, 1024], P('row'), may hold values from -1 to 2, as said below
- occ_energy: float32 [96], replicated, may hold values from -3 to -0.5
- vir_energy: float32 [256], replicated, may hold values from 0.2 to 4
- orbital_slot: int32 [96], replicated, may hold values from 0 to 95, each once
- source_plan: int32 [2, 2, 4], P('row'), may hold values from 0 to 95, as said below
- pair_list: int32 [2, 16, 2, 24], P('row', 'col'), may hold values from -1 to 23, as said below
Outputs:
- gamma_fit: float32 [2, 256, 8, 1024], P('row', 'col')
Inputs may be any that keep to these rules, and one draw needn't show every extreme that they name: `metric_root`: Symmetric. `source_plan`: all entries are distinct orbitals. `pair_list`: each list holds 2 to 24 distinct codes k * 6 + l first and -1 in the remaining entries; in every draw some list is full.
All inputs are finite; a program needn't handle non-finite values.
Results may differ from a plain program's by a relative error of at most 0.003.
Values may be sent and summed in bfloat16 or wider, within the bound.
A program may use at most 128 MiB of HBM per device.

v0:
```python
from functools import partial

import jax
import jax.numpy as jnp
from jax import lax
from jax.sharding import PartitionSpec as P


def from_root(shard, axis, root):
    mine = lax.axis_index(axis) == root
    return lax.psum(jnp.where(mine, shard, jnp.zeros_like(shard)), axis)


def fetch_factor(factors, slot_index, owned_slots):
    holder = slot_index // owned_slots
    position = slot_index % owned_slots
    portion = lax.dynamic_index_in_dim(factors, position, 0, keepdims=False)
    return from_root(portion, "col", holder)


def masked_weights(sources, factors, source_energy, local_energy, vir_energy, pair_mask):
    integrals = jnp.einsum("kaq,lbq->klab", sources, factors, preferred_element_type=jnp.float32)
    denominator = (
        source_energy[:, None, None, None]
        + local_energy[None, :, None, None]
        - vir_energy[None, None, :, None]
        - vir_energy[None, None, None, :]
    )
    amplitude = integrals / denominator
    return ((2.0 * amplitude - jnp.swapaxes(amplitude, 2, 3)) * pair_mask[:, :, None, None]).astype(
        jnp.bfloat16
    )


def contract_rows(weights, factors, offset, length):
    return jnp.einsum("klab,lbq->akq", weights, factors, preferred_element_type=jnp.float32)


def fold_metric(flat_gamma, portion):
    return jnp.dot(flat_gamma, portion, preferred_element_type=jnp.float32)


def on_device(factors, metric_root, occ_energy, vir_energy, orbital_slot, source_plan, pair_list):
    owned_slots = factors.shape[0]
    virtual = factors.shape[1]
    aux_count = factors.shape[2]
    columns = lax.axis_size("col")
    steps_count = source_plan.shape[1]
    sources_count = source_plan.shape[2]
    occupied = occ_energy.shape[0]
    column = lax.axis_index("col")
    local_slots = column * owned_slots + jnp.arange(owned_slots, dtype=jnp.int32)
    local_match = orbital_slot[None, :] == local_slots[:, None]
    local_energy = jnp.sum(jnp.where(local_match, occ_energy[None, :], 0.0), axis=1)
    source_match = (
        source_plan[0][:, :, None] == jnp.arange(occupied, dtype=jnp.int32)[None, None, :]
    )
    source_energy = jnp.sum(jnp.where(source_match, occ_energy[None, None, :], 0.0), axis=2)
    source_slot = jnp.sum(jnp.where(source_match, orbital_slot[None, None, :], 0), axis=2)
    code_range = jnp.arange(sources_count * owned_slots, dtype=jnp.int32)
    share_rows = virtual // columns
    makers = []
    for s in range(steps_count):
        sources = jnp.stack(
            [fetch_factor(factors, source_slot[s, k], owned_slots) for k in range(sources_count)]
        )
        code_list = pair_list[0, 0, s]
        pair_mask = (
            jnp.any(code_list[:, None] == code_range[None, :], axis=0)
            .reshape(sources_count, owned_slots)
            .astype(jnp.float32)
        )
        weights = masked_weights(
            sources, factors, source_energy[s], local_energy, vir_energy, pair_mask
        )
        term = partial(contract_rows, weights, factors)
        makers.append(term)
    offset = jnp.int32(0)
    gamma_rows = lax.psum_scatter(
        jnp.concatenate(
            [maker(offset, share_rows * lax.axis_size("col")) for maker in makers], axis=1
        ),
        "col",
        scatter_dimension=0,
        tiled=True,
    )
    flat_gamma = gamma_rows.astype(jnp.bfloat16).reshape(
        share_rows * steps_count * sources_count, aux_count
    )
    fitted = fold_metric(flat_gamma, lax.all_gather(metric_root, "row", axis=0, tiled=True))
    return fitted.reshape(1, share_rows, steps_count * sources_count, aux_count)


def solution(mesh):
    in_specs = (
        P("col", None, None),
        P("row", None),
        P(),
        P(),
        P(),
        P("row", None, None),
        P("row", "col", None, None),
    )
    out_specs = P("row", "col", None, None)
    return jax.shard_map(
        on_device, mesh=mesh, in_specs=in_specs, out_specs=out_specs, check_vma=False
    )
```

profile of v0, /device:TPU:0, one launch (start us, length us, event | category | flops | bytes accessed | tf_op | source)
XLA Modules:
  0.0 309.6 jit_solution(2107653622613330632)
XLA Ops:
  7.4 0.9 select_reduce_fusion.2
  8.3 0.7 fusion.42
  24.3 4.2 %dynamic-slice_select_fusion.7 = (bf16[1,256,1024]{2,1,0:T(8,128)(2,1)}, bf16[1,256,1024]{2,1,0:T(8,128)(2,1)}, bf16[1,256,1024]{2,1,0:T(8,128)(2,1)}, bf16[1,25...) fusion(bf16[6,256,1024]{2,1,0:T(8,128)(2,1)} %param.7, ...), kind=kLoop, calls=%fused_computation.47 | loop fusion | flops 2097152 | bytes 8388648 | tf_op jit(solution)/shard_map/jit(_where)/select_n | solution.py:11
  28.6 0.0 copy-start.3
  28.6 0.0 copy-start.6
  28.6 0.0 copy-start.5
  28.6 0.0 copy-start.1
  28.6 0.0 all-reduce.3.cloned.1.call-update
  28.6 0.0 all-gather.2.cloned.1.call-start
  28.7 0.5 all-gather.2.cloned.1.call-update
  29.2 0.0 reduce-scatter.2.cloned.1.call-start
  29.3 0.2 select_reduce_fusion.1
  29.5 0.2 select_reduce_fusion
  29.7 0.1 fusion.36
  29.8 0.1 reshape.200
  29.9 0.1 reshape.201
  29.9 0.1 broadcast_add_fusion.1
  30.0 0.1 broadcast_subtract_fusion.1
  30.1 113.5 %all-reduce.3.cloned.1.call-done = (bf16[1,256,1024]{2,1,0:T(8,128)(2,1)}, bf16[1,256,1024]{2,1,0:T(8,128)(2,1)}, bf16[1,256,1024]{2,1,0:T(8,128)(2,1)}, bf16[1,...) async-done(((bf16[1,256,1024]{2,1,0:T(8,128)(2,1)}, ...) | async-done | bytes 4194320 | tf_op jit(solution)/shard_map/psum | solution.py:11
  143.6 6.8 %fusion.14 = f32[4,256,6,256]{3,1,2,0:T(8,128)} fusion(bf16[6,256,1024]{2,1,0:T(8,128)(2,1)S(1)} %copy-done.1, bf16[1,256,1024]{2,1,0:T(8,128)(2,1)} %get-tuple-element.9, bf16[1,256,1024]{2,1,0:T(8,128)(2,1)} %get-tuple-element.10, bf16[1,256,1024]{2,1,0:T(8,128)(2,1)} %get-tuple-element.11, bf16[1,256,1024]{2,1,0:T(8,128)(2,1)} %get-tuple-element.12), kind=kOutput, calls=%fused_computation.21 | convolution fusion | flops 3229614080 | bytes 11534336 | tf_op jit(solution)/shard_map/kaq,lbq->klab/dot_general | solution.py:22
  150.5 6.5 %copy.10 = f32[4,256,6,256]{1,3,2,0:T(8,128)} copy(f32[4,256,6,256]{3,1,2,0:T(8,128)} %fusion.14) | data formatting | bytes 12582912 | tf_op jit(solution)/shard_map/kaq,lbq->klab/dot_general | solution.py:22
  157.0 7.2 %fusion.12 = f32[4,256,1024,1]{2,1,3,0:T(8,128)S(1)} fusion(bf16[6,256,1024]{2,1,0:T(8,128)(2,1)S(1)} %copy-done.1, f32[4,256,6,256]{3,1,2,0:T(8,128)} %fusion.14, f32[4,256,6,256]{1,3,2,0:T(8,128)} %copy.10, f32[4,6]{1,0:T(4,128)S(1)} %reshape.200, f32[256]{0:T(256)S(1)} %copy-done.5, f32[4,6,256]{2,1,0:T(8,128)S(1)} %get-tuple-element.21), kind=kOutput, calls=%fused_computation.19 | convolution fusion | flops 3233808384 | bytes 19948640 | tf_op jit(solution)/shard_map/klab,lbq->akq/dot_general | solution.py:36
  164.3 4.6 %copy.19 = f32[4,256,1024,1]{2,0,1,3:T(4,128)} copy(f32[4,256,1024,1]{2,1,3,0:T(8,128)S(1)} %fusion.12) | data formatting | bytes 8388608 | tf_op jit(solution)/shard_map/klab,lbq->akq/dot_general | solution.py:36
  168.9 5.3 %fusion.10 = f32[4,256,6,256]{3,1,2,0:T(8,128)} fusion(bf16[6,256,1024]{2,1,0:T(8,128)(2,1)S(1)} %copy-done.1, bf16[1,256,1024]{2,1,0:T(8,128)(2,1)S(1)} %copy-done.7, bf16[1,256,1024]{2,1,0:T(8,128)(2,1)S(1)} %copy-done.8, bf16[1,256,1024]{2,1,0:T(8,128)(2,1)S(1)} %copy-done.9, bf16[1,256,1024]{2,1,0:T(8,128)(2,1)S(1)} %copy-done.10), kind=kOutput, calls=%fused_computation.17 | convolution fusion | flops 3229614080 | bytes 11534336 | tf_op jit(solution)/shard_map/kaq,lbq->klab/dot_general | solution.py:22
  174.3 6.5 %copy.11 = f32[4,256,6,256]{1,3,2,0:T(8,128)} copy(f32[4,256,6,256]{3,1,2,0:T(8,128)} %fusion.10) | data formatting | bytes 12582912 | tf_op jit(solution)/shard_map/kaq,lbq->klab/dot_general | solution.py:22
  180.8 7.4 %fusion.8 = f32[4,256,1024,1]{2,1,3,0:T(8,128)S(1)} fusion(bf16[6,256,1024]{2,1,0:T(8,128)(2,1)S(1)} %copy-done.1, f32[4,256,6,256]{3,1,2,0:T(8,128)} %fusion.10, f32[4,256,6,256]{1,3,2,0:T(8,128)} %copy.11, f32[4,6]{1,0:T(4,128)S(1)} %reshape.201, f32[4,6,256]{2,1,0:T(8,128)S(1)} %get-tuple-element.22, f32[256]{0:T(256)S(1)} %copy-done.5), kind=kOutput, calls=%fused_computation.15 | convolution fusion | flops 3233808384 | bytes 19948640 | tf_op jit(solution)/shard_map/klab,lbq->akq/dot_general | solution.py:36
  188.2 2.7 copy.18
  191.0 5.4 %pad_maximum_fusion = f32[256,8,1024]{2,1,0:T(8,128)} fusion(f32[256,4,1024]{2,1,0:T(4,128)S(1)} %bitcast.102, f32[256,4,1024]{2,1,0:T(4,128)S(1)} %bitcast.101), kind=kLoop, calls=%fused_computation | loop fusion | flops 2097152 | bytes 16777216 | tf_op jit(solution)/shard_map/concatenate | solution.py:80
  196.3 0.0 reduce-scatter.2.cloned.1.call-update
  196.3 0.0 all-gather.2.cloned.1.call-done
  196.4 102.8 %reduce-scatter.2.cloned.1.call-done = f32[16,8,1024]{2,1,0:T(8,128)} async-done(((f32[256,8,1024]{2,1,0:T(8,128)}), f32[16,8,1024]{2,1,0:T(8,128)}) %reduce-scatter.2.cloned.1.call-update) | async-done | bytes 524304 | tf_op jit(solution)/shard_map/reduce_scatter | solution.py:79
  299.2 3.0 fusion.32
  (24 shorter events, 0.1 us)
Async XLA Ops:
  7.4 136.3 %all-reduce.3.cloned.1.call-start = ((), (), s32[]{:S(2)}) async-start(), calls=%async_computation.3 | async-start | bytes 8388608 | tf_op jit(solution)/shard_map/psum | solution.py:11
  28.6 0.7 copy-start.2
  28.6 0.7 copy-start.4
  28.6 0.9 copy-start.3
  28.6 1.1 copy-start.6
  28.6 1.4 copy-start.5
  28.6 115.0 %copy-start.1 = (bf16[6,256,1024]{2,1,0:T(8,128)(2,1)S(1)}, bf16[6,256,1024]{2,1,0:T(8,128)(2,1)}, u32[]{:S(2)}) copy-start(bf16[6,256,1024]{2,1,0:T(8,128)(2,1)} %param.7) | copy-start | bytes 9437188
  28.6 167.7 %all-gather.2.cloned.1.call-start = ((), (), s32[]{:S(2)}) async-start(), calls=%async_computation.2 | async-start | bytes 3145728 | tf_op jit(solution)/shard_map/all_gather | solution.py:90
  29.2 270.0 %reduce-scatter.2.cloned.1.call-start = ((), (), s32[]{:S(2)}) async-start(), calls=%async_computation.1 | async-start | bytes 8912896 | tf_op jit(solution)/shard_map/reduce_scatter | solution.py:79
  164.3 4.7 %copy-start.7 = (bf16[1,256,1024]{2,1,0:T(8,128)(2,1)S(1)}, bf16[1,256,1024]{2,1,0:T(8,128)(2,1)}, u32[]{:S(2)}) copy-start(bf16[1,256,1024]{2,1,0:T(8,128)(2,1)} %get-tuple-element.5) | copy-start | bytes 1572868
  164.3 4.7 %copy-start.8 = (bf16[1,256,1024]{2,1,0:T(8,128)(2,1)S(1)}, bf16[1,256,1024]{2,1,0:T(8,128)(2,1)}, u32[]{:S(2)}) copy-start(bf16[1,256,1024]{2,1,0:T(8,128)(2,1)} %get-tuple-element.6) | copy-start | bytes 1572868
  164.3 4.7 %copy-start.9 = (bf16[1,256,1024]{2,1,0:T(8,128)(2,1)S(1)}, bf16[1,256,1024]{2,1,0:T(8,128)(2,1)}, u32[]{:S(2)}) copy-start(bf16[1,256,1024]{2,1,0:T(8,128)(2,1)} %get-tuple-element.7) | copy-start | bytes 1572868
  164.3 4.7 %copy-start.10 = (bf16[1,256,1024]{2,1,0:T(8,128)(2,1)S(1)}, bf16[1,256,1024]{2,1,0:T(8,128)(2,1)}, u32[]{:S(2)}) copy-start(bf16[1,256,1024]{2,1,0:T(8,128)(2,1)} %get-tuple-element.8) | copy-start | bytes 1572868
  188.2 2.7 copy-start
Sparse Core Ops, SparseCore 0:
  28.8 114.8 all-reduce.2
  196.5 102.6 reduce-scatter.1
Sparse Core Ops, SparseCore 1:
  30.7 35.7 all-gather.1
where the time goes:
time: 310 us
  waiting for transfers between devices  217 us (70%)
  between operations  30.4 us (10%)
  matrix products  29.8 us (10%)
  local copies, waits for them, and re-layouts  21.3 us (7%)
  other arithmetic  11.1 us (4%)
    psum x1, waiting for transfers between devices, from_root(): return lax.psum(jnp.where(mine, shard, jnp.zeros_like(shard)), axis)  114 us
    reduce_scatter x1, waiting for transfers between devices, on_device(): lax.psum_scatter(jnp.concatenate([maker(offset, share_rows * lax.axis_siz...  103 us
    dot_general x2, matrix products, contract_rows(): jnp.einsum('klab,lbq->akq', weights, factors, preferred_element_type=jnp....  14.6 us
    dot_general x2, local copies, waits for them, and re-layouts, masked_weights(): jnp.einsum('kaq,lbq->klab', sources, factors, preferred_element_type=jnp....  13.1 us
    dot_general x2, matrix products, masked_weights(): jnp.einsum('kaq,lbq->klab', sources, factors, preferred_element_type=jnp....  12.2 us
    dot_general x2, local copies, waits for them, and re-layouts, contract_rows(): jnp.einsum('klab,lbq->akq', weights, factors, preferred_element_type=jnp....  7.33 us
  transfers between devices with their start and end apart: 3, of which 2 were waited for; matrix products, arithmetic and copies ran while one was open for 17% of the time, Pallas kernels for 0%

commit v1 on v0

v1 whole, which is shorter than its diff:
```python
from functools import partial

import jax
import jax.numpy as jnp
from jax import lax
from jax.experimental import pallas as pl
from jax.experimental.pallas import tpu as pltpu
from jax.sharding import PartitionSpec as P

MESH = pl.DeviceIdType.MESH
BF = jnp.bfloat16
F32 = jnp.float32

D_CORE, D_YRS, D_ZRS, D_ZAG, D_YAG, D_CAG, D_COMP = 0, 1, 2, 3, 4, 5, 6
D_GY, D_GZ, D_GEND = 7, 8, 9


def kernel(
    dims,
    pos_ref, flag_ref, esrc_ref, eloc_ref, mask_ref,
    f_ref, metric_ref, vcol_ref, vrow_ref,
    out_ref,
    own, c_in, t1, y_in, t2, z_in, full,
    wbuf, gsum, gc_out, gc_in, gmid, gy_out, gy_in, gz_out, gz_in, acc, mroot,
    s_c, r_c, s_y, r_y, s_z, r_z, s_za, r_za, s_ya, r_ya, s_ca, r_ca,
    s_gc, r_gc, s_gy, r_gy, s_gz, r_gz, s_m, r_m, l_m,
):
    K, A, B, NR, O, V, NP = dims
    HV = V // 2
    YV = HV // B
    ZP = NP // A
    R = V // (2 * A * B)
    row = lax.axis_index("row")
    col = lax.axis_index("col")
    h = lax.rem(col, 2)
    chip = col // 2
    y = lax.rem(chip, B)
    z = chip // B

    def at(zz, yy, hh):
        return (row, (zz * B + yy) * 2 + hh)

    partner = at(z, y, 1 - h)

    def ypeer(d):
        return lax.rem(y + d, B)

    def yfrom(d):
        return lax.rem(y + B - d, B)

    def zpeer(d):
        return lax.rem(z + d, A)

    def zfrom(d):
        return lax.rem(z + A - d, A)

    def rcopy(src, dst, ss, rs, dev):
        return pltpu.make_async_remote_copy(
            src_ref=src, dst_ref=dst, send_sem=ss, recv_sem=rs, device_id=dev, device_id_type=MESH
        )

    barrier = pltpu.get_barrier_semaphore()
    peers = [partner]
    peers += [at(z, ypeer(d), h) for d in range(1, B)]
    peers += [at(zpeer(d), y, h) for d in range(1, A)]
    peers += [(lax.rem(row + d, NR), col) for d in range(1, NR)]
    for dev in peers:
        pl.semaphore_signal(barrier, inc=1, device_id=dev, device_id_type=MESH)
    pl.semaphore_wait(barrier, len(peers))

    def m_copy(d):
        return rcopy(
            metric_ref, mroot.at[row], s_m.at[d - 1], r_m.at[d - 1], (lax.rem(row + d, NR), col)
        )

    m_local = pltpu.make_async_copy(metric_ref, mroot.at[row], l_m)
    m_local.start()

    hrow = pl.multiple_of(h * HV, HV)
    orow = pl.multiple_of((1 - h) * HV, HV)

    def lanes(zz):
        return pl.ds(pl.multiple_of(zz * ZP, ZP), ZP)

    def yrows(yy):
        return pl.ds(pl.multiple_of(yy * YV, YV), YV)

    def frows(yy):
        return pl.ds(pl.multiple_of(h * HV + yy * YV, YV), YV)

    def core_rs(k):
        return rcopy(own.at[k], c_in.at[k], s_c.at[k], r_c.at[k], partner)

    def y_rs(k, d):
        return rcopy(
            t1.at[k, yrows(ypeer(d))], y_in.at[k, d - 1], s_y.at[k, d - 1], r_y.at[k, d - 1],
            at(z, ypeer(d), h),
        )

    def z_rs(k, d):
        return rcopy(
            t2.at[k, :, lanes(zpeer(d))], z_in.at[k, d - 1], s_z.at[k, d - 1], r_z.at[k, d - 1],
            at(zpeer(d), y, h),
        )

    def z_ag(k, d):
        piece = full.at[k, frows(y), lanes(z)]
        return rcopy(piece, piece, s_za.at[k, d - 1], r_za.at[k, d - 1], at(zpeer(d), y, h))

    def z_ag_in(k, d):
        piece = full.at[k, frows(y), lanes(zfrom(d))]
        return rcopy(piece, piece, s_za.at[k, d - 1], r_za.at[k, d - 1], at(zpeer(d), y, h))

    def y_ag(k, d):
        piece = full.at[k, frows(y)]
        return rcopy(piece, piece, s_ya.at[k, d - 1], r_ya.at[k, d - 1], at(z, ypeer(d), h))

    def y_ag_in(k, d):
        piece = full.at[k, frows(yfrom(d))]
        return rcopy(piece, piece, s_ya.at[k, d - 1], r_ya.at[k, d - 1], at(z, ypeer(d), h))

    def c_ag(k):
        piece = full.at[k, pl.ds(hrow, HV)]
        return rcopy(piece, piece, s_ca.at[k], r_ca.at[k], partner)

    def c_ag_in(k):
        piece = full.at[k, pl.ds(orow, HV)]
        return rcopy(piece, piece, s_ca.at[k], r_ca.at[k], partner)

    def g_core(k):
        return rcopy(gc_out.at[k], gc_in.at[k], s_gc.at[k], r_gc.at[k], partner)

    def g_y(k, d):
        return rcopy(
            gy_out.at[k, d - 1], gy_in.at[k, d - 1], s_gy.at[k, d - 1], r_gy.at[k, d - 1],
            at(z, ypeer(d), h),
        )

    def g_z(k, d):
        return rcopy(
            gz_out.at[k, d - 1], gz_in.at[k, d - 1], s_gz.at[k, d - 1], r_gz.at[k, d - 1],
            at(zpeer(d), y, h),
        )

    def flagged(k, start):
        flag = jnp.full((HV, NP), flag_ref[k], F32).astype(BF)
        return f_ref[pos_ref[k], pl.ds(start, HV), :] * flag

    def st_core(k):
        own[k] = flagged(k, orow)
        core_rs(k).start()

    def st_yrs(k):
        core_rs(k).wait_recv()
        t1[k] = flagged(k, hrow) + c_in[k]
        for d in range(1, B):
            y_rs(k, d).start()

    def st_zrs(k):
        total = t1[k, yrows(y), :]
        for d in range(1, B):
            y_rs(k, d).wait_recv()
            total = total + y_in[k, d - 1]
        t2[k] = total
        for d in range(1, A):
            z_rs(k, d).start()

    def st_zag(k):
        total = t2[k, :, lanes(z)]
        for d in range(1, A):
            z_rs(k, d).wait_recv()
            total = total + z_in[k, d - 1]
        full[k, frows(y), lanes(z)] = total
        for d in range(1, A):
            z_ag(k, d).start()

    def st_yag(k):
        for d in range(1, A):
            z_ag_in(k, d).wait_recv()
        for d in range(1, B):
            y_ag(k, d).start()

    def st_cag(k):
        for d in range(1, B):
            y_ag_in(k, d).wait_recv()
        c_ag(k).start()

    def st_comp(k):
        c_ag_in(k).wait_recv()
        source = full[k]
        for l in range(O):
            ints = lax.dot_general(
                source, f_ref[l], (((1,), (1,)), ((), ())), preferred_element_type=F32
            )
            top = 2.0 * ints - jnp.transpose(ints)
            den = (esrc_ref[k] + eloc_ref[l] - vcol_ref[...]) - vrow_ref[...]
            wbuf[:, l * V:(l + 1) * V] = (top / den * mask_ref[k * O + l]).astype(BF)
        gamma = jnp.dot(
            wbuf[...], f_ref[...].reshape(O * V, NP), preferred_element_type=F32
        )
        gsum[k] = gamma.reshape(A, B, 2, R, NP)
        gc_out[k] = gsum[k, :, :, 1 - h].astype(BF)
        g_core(k).start()

    def st_gy(k):
        g_core(k).wait_recv()
        gmid[k] = gsum[k, :, :, h] + gc_in[k].astype(F32)
        for d in range(1, B):
            gy_out[k, d - 1] = gmid[k, :, ypeer(d)].astype(BF)
            g_y(k, d).start()

    def st_gz(k):
        for d in range(1, B):
            g_y(k, d).wait_recv()
            gmid[k, :, y] = gmid[k, :, y] + gy_in[k, d - 1].astype(F32)
        for d in range(1, A):
            gz_out[k, d - 1] = gmid[k, zpeer(d), y].astype(BF)
            g_z(k, d).start()

    def st_gend(k):
        total = gmid[k, z, y]
        for d in range(1, A):
            g_z(k, d).wait_recv()
            total = total + gz_in[k, d - 1].astype(F32)
        acc[k] = total

    stages = (
        (D_CORE, st_core), (D_YRS, st_yrs), (D_ZRS, st_zrs), (D_ZAG, st_zag), (D_YAG, st_yag),
        (D_CAG, st_cag), (D_GEND, st_gend), (D_GZ, st_gz), (D_GY, st_gy), (D_COMP, st_comp),
    )

    def tick(t, carry):
        for delay, stage in stages:
            k = t - delay
            pl.when((k >= 0) & (k < K))(partial(stage, k))

        @pl.when(t == 2)
        def _():
            for d in range(1, NR):
                m_copy(d).start()

        return carry

    lax.fori_loop(0, K + D_GEND, tick, 0)

    m_local.wait()
    for d in range(1, NR):
        m_copy(d).wait()
    root = mroot[...].reshape(NP, NP)
    gamma = acc[...].reshape(K * R, NP)
    high = gamma.astype(BF)
    low = (gamma - high.astype(F32)).astype(BF)
    fitted = jnp.dot(high, root, preferred_element_type=F32)
    fitted = fitted + jnp.dot(low, root, preferred_element_type=F32)
    out_ref[...] = fitted.reshape(K, R, NP)

    def drain(k, carry):
        core_rs(k).wait_send()
        for d in range(1, B):
            y_rs(k, d).wait_send()
            y_ag(k, d).wait_send()
            g_y(k, d).wait_send()
        for d in range(1, A):
            z_rs(k, d).wait_send()
            z_ag(k, d).wait_send()
            g_z(k, d).wait_send()
        c_ag(k).wait_send()
        g_core(k).wait_send()
        return carry

    lax.fori_loop(0, K, drain, 0)


def on_device(factors, metric_root, occ_energy, vir_energy, orbital_slot, source_plan, pair_list):
    O, V, NP = factors.shape
    n = lax.axis_size("col")
    NR = lax.axis_size("row")
    chips = n // 2
    A = 4 if chips % 4 == 0 else chips
    B = chips // A
    steps, sources = source_plan.shape[1:]
    K = steps * sources
    R = V // n
    HV, YV, ZP = V // 2, V // 2 // B, NP // A
    column = lax.axis_index("col")
    occupied = occ_energy.shape[0]
    local_slots = column * O + jnp.arange(O, dtype=jnp.int32)
    local_match = orbital_slot[None, :] == local_slots[:, None]
    local_energy = jnp.sum(jnp.where(local_match, occ_energy[None, :], 0.0), axis=1)
    plan = source_plan.reshape(K)
    source_match = plan[:, None] == jnp.arange(occupied, dtype=jnp.int32)[None, :]
    source_energy = jnp.sum(jnp.where(source_match, occ_energy[None, :], 0.0), axis=1)
    source_slot = jnp.sum(jnp.where(source_match, orbital_slot[None, :], 0), axis=1)
    position = (source_slot % O).astype(jnp.int32)
    flag = (source_slot // O == column).astype(F32)
    codes = jnp.arange(sources * O, dtype=jnp.int32)
    pair_mask = jnp.any(
        pair_list.reshape(steps, -1)[:, :, None] == codes[None, None, :], axis=1
    ).astype(F32).reshape(K * O)

    dma = pltpu.SemaphoreType.DMA
    b1, a1 = max(B - 1, 1), max(A - 1, 1)
    per_k = (K,)
    sems = []
    for shape in (per_k, (K, b1), (K, a1), (K, a1), (K, b1), per_k, per_k, (K, b1), (K, a1)):
        sems += [dma(shape), dma(shape)]
    nr1 = max(NR - 1, 1)
    sems += [dma((nr1,)), dma((nr1,)), dma]
    vm = pltpu.VMEM
    out = pl.pallas_call(
        partial(kernel, (K, A, B, NR, O, V, NP)),
        out_shape=jax.ShapeDtypeStruct((K, R, NP), F32),
        in_specs=[pl.BlockSpec(memory_space=pltpu.SMEM)] * 5 + [pl.BlockSpec(memory_space=vm)] * 4,
        out_specs=pl.BlockSpec(memory_space=vm),
        scratch_shapes=[
            vm((K, HV, NP), BF),
            vm((K, HV, NP), BF),
            vm((K, HV, NP), BF),
            vm((K, b1, YV, NP), BF),
            vm((K, YV, NP), BF),
            vm((K, a1, YV, ZP), BF),
            vm((K, V, NP), BF),
            vm((V, O * V), BF),
            vm((K, A, B, 2, R, NP), F32),
            vm((K, A, B, R, NP), BF),
            vm((K, A, B, R, NP), BF),
            vm((K, A, B, R, NP), F32),
            vm((K, b1, A, R, NP), BF),
            vm((K, b1, A, R, NP), BF),
            vm((K, a1, R, NP), BF),
            vm((K, a1, R, NP), BF),
            vm((K, R, NP), F32),
            vm((NR, NP // NR, NP), BF),
        ] + sems,
        compiler_params=pltpu.CompilerParams(
            collective_id=0, has_side_effects=True, vmem_limit_bytes=60 * 1024 * 1024
        ),
    )(
        position, flag, source_energy, local_energy, pair_mask,
        factors, metric_root, vir_energy[:, None], vir_energy[None, :],
    )
    return jnp.transpose(out, (1, 0, 2))[None]


def solution(mesh):
    in_specs = (
        P("col", None, None),
        P("row", None),
        P(),
        P(),
        P(),
        P("row", None, None),
        P("row", "col", None, None),
    )
    out_specs = P("row", "col", None, None)
    return jax.shard_map(
        on_device, mesh=mesh, in_specs=in_specs, out_specs=out_specs, check_vma=False
    )
```

time: 310 us -> 109 us (0.35)
  waiting for transfers between devices: 217 us -> 0 us
  Pallas kernels: 0 us -> 97.9 us
  between operations: 30.4 us -> 0.01 us
  matrix products: 29.8 us -> 0 us
  local copies, waits for them, and re-layouts: 21.3 us -> 4.96 us
  other arithmetic: 11.1 us -> 5.54 us
    psum x1 -> x0, waiting for transfers between devices: 114 us -> none  [from_root(): return lax.psum(jnp.where(mine, shard, jnp.zeros_like(shard)), axis)]
    reduce_scatter x1 -> x0, waiting for transfers between devices: 103 us -> none  [on_device(): lax.psum_scatter(jnp.concatenate([maker(offset, share_rows * lax.axis_siz...]
    pallas_call x0 -> x1, Pallas kernels: none -> 97.9 us  [on_device(): pl.pallas_call(partial(kernel, (K, A, B, NR, O, V, NP)), out_shape=jax.Sh...]
    dot_general x5 -> x0, matrix products: 29.8 us -> none  [the longest x2 14.6 us: contract_rows(): jnp.einsum('klab,lbq->akq', weights, factors, preferred_element_type=jnp....]
    dot_general x4 -> x0, local copies, waits for them, and re-layouts: 20.4 us -> none  [the longest x2 13.1 us: masked_weights(): jnp.einsum('kaq,lbq->klab', sources, factors, preferred_element_type=jnp....]
    concatenate x1 -> x0, other arithmetic: 5.37 us -> none  [on_device(): jnp.concatenate([maker(offset, share_rows * lax.axis_size('col')) for mak...]
    broadcast_in_dim x0 -> x2, local copies, waits for them, and re-layouts: none -> 3.61 us  [the longest x1 2.14 us: on_device(): return jnp.transpose(out, (1, 0, 2))[None]]
    select_n x1, other arithmetic: 4.21 us -> 0.6 us  [on_device(): position = (source_slot % O).astype(jnp.int32)]
  transfers between devices with their start and end apart: 3 -> 0, of which waited for: 2 -> 0; matrix products, arithmetic and copies ran while one was open for 17% -> 0% of each run, Pallas kernels for 0% -> 0%
where the time goes in v1:
time: 109 us; the launch traced here: 108 us
  Pallas kernels  97.9 us (90%)
  other arithmetic  5.54 us (5%)
  local copies, waits for them, and re-layouts  4.96 us (5%)
    pallas_call x1, Pallas kernels, on_device(): pl.pallas_call(partial(kernel, (K, A, B, NR, O, V, NP)), out_shape=jax.Sh...  97.9 us

profile of v1, /device:TPU:0, one launch (start us, length us, event | category | flops | bytes accessed | tf_op | source)
XLA Modules:
  0.0 108.4 jit_solution(6154766638080775875)
XLA Ops:
  0.0 1.4 %select_reduce_fusion.eloc_ref = f32[6]{0:T(128)} fusion(f32[96]{0:T(128)} %param.9, s32[96]{0:T(128)} %param.11, s32[6]{0:T(128)S(1)} %iota_add_fusion), kind=kLoop, calls=%fused_computation.2 | loop fusion | flops 1722 | bytes 816 | tf_op jit(solution)/shard_map/reduce_sum | solution.py:289
  1.4 0.8 eq.51
  2.2 0.8 select_reduce_fusion.2
  3.0 1.4 %select_reduce_fusion.1.esrc_ref = f32[8]{0:T(128)} fusion(f32[96]{0:T(128)} %param.9, s32[8]{0:T(128)S(1)} %eq.51), kind=kLoop, calls=%fused_computation.3 | loop fusion | flops 2296 | bytes 448 | tf_op jit(solution)/shard_map/reduce_sum | solution.py:292
  4.4 0.5 compare_convert_fusion.flag_ref
  4.9 0.6 and_select_fusion.1.pos_ref
  5.5 0.8 fusion
  6.3 0.6 reshape.12.mask_ref
  6.9 1.5 %copy.11.vcol_ref = f32[256,1]{1,0:T(8,128)} copy(f32[256,1]{0,1:T(1,128)} %bitcast.7) | data formatting | bytes 2048 | tf_op jit(solution)/shard_map/broadcast_in_dim | solution.py:340
  8.4 97.9 %shard_map.73 = f32[8,16,1024]{2,1,0:T(8,128)} custom-call(s32[8]{0:T(128)} %and_select_fusion.1.pos_ref, f32[8]{0:T(128)} %compare_convert_fusion.flag_ref, f32[8]{0:T(128)} %select_reduce_fusion.1.esrc_ref, f32[6]{0:T(128)} %select_reduce_fusion.eloc_ref, f32[48]{0:T(128)} %reshape.12.mask_ref, bf16[6,256,1024]{2,1,0:T(8,128)(2,1)} %f_ref.1, ...), custom_call_target="tpu_custom_call" | custom-call | tf_op jit(solution)/shard_map/pallas_call | solution.py:310
  106.2 2.1 %copy.12 = f32[1,16,8,1024]{3,2,1,0:T(8,128)} copy(f32[1,16,8,1024]{3,1,2,0:T(8,128)} %bitcast.6) | data formatting | bytes 1048576 | tf_op jit(solution)/shard_map/broadcast_in_dim | solution.py:342
  (2 shorter events, 0.0 us)

commit v2 on v1

--- a/solution.py
+++ b/solution.py
@@ -11,21 +11,19 @@
 BF = jnp.bfloat16
 F32 = jnp.float32
 
-D_CORE, D_YRS, D_ZRS, D_ZAG, D_YAG, D_CAG, D_COMP = 0, 1, 2, 3, 4, 5, 6
-D_GY, D_GZ, D_GEND = 7, 8, 9
-
-
 def kernel(
     dims,
-    pos_ref, flag_ref, esrc_ref, eloc_ref, mask_ref,
-    f_ref, metric_ref, vcol_ref, vrow_ref,
+    plan_ref, slot_ref, occ_ref,
+    f_ref, metric_ref, vrow_ref, slots_ref, occs_ref, pairs_ref,
     out_ref,
-    own, c_in, t1, y_in, t2, z_in, full,
+    own, c_in, t1, y_in, t2, rin, rout, lin, lout, zr_in, zr_out, zl_in, zl_out, zy_out, zy_in, full,
+    vsum, eloc,
     wbuf, gsum, gc_out, gc_in, gmid, gy_out, gy_in, gz_out, gz_in, acc, mroot,
-    s_c, r_c, s_y, r_y, s_z, r_z, s_za, r_za, s_ya, r_ya, s_ca, r_ca,
+    s_c, r_c, s_y, r_y, s_r, r_r, s_l, r_l, s_zr, r_zr, s_zl, r_zl, s_zy, r_zy, s_ar, r_ar, s_al, r_al,
+    s_ya, r_ya, s_ca, r_ca,
     s_gc, r_gc, s_gy, r_gy, s_gz, r_gz, s_m, r_m, l_m,
 ):
-    K, A, B, NR, O, V, NP = dims
+    K, A, B, NR, O, V, NP, SRC = dims
     HV = V // 2
     YV = HV // B
     ZP = NP // A
@@ -97,19 +95,39 @@
             at(z, ypeer(d), h),
         )
 
-    def z_rs(k, d):
-        return rcopy(
-            t2.at[k, :, lanes(zpeer(d))], z_in.at[k, d - 1], s_z.at[k, d - 1], r_z.at[k, d - 1],
-            at(zpeer(d), y, h),
-        )
-
-    def z_ag(k, d):
-        piece = full.at[k, frows(y), lanes(z)]
-        return rcopy(piece, piece, s_za.at[k, d - 1], r_za.at[k, d - 1], at(zpeer(d), y, h))
-
-    def z_ag_in(k, d):
-        piece = full.at[k, frows(y), lanes(zfrom(d))]
-        return rcopy(piece, piece, s_za.at[k, d - 1], r_za.at[k, d - 1], at(zpeer(d), y, h))
+    right, left = at(lax.rem(z + 1, A), y, h), at(lax.rem(z + A - 1, A), y, h)
+
+    def sweep_r(k):
+        return rcopy(rout.at[k], rin.at[k], s_r.at[k], r_r.at[k], right)
+
+    def sweep_l(k):
+        return rcopy(lout.at[k], lin.at[k], s_l.at[k], r_l.at[k], left)
+
+    def chain_r(k, d):
+        cut = pl.ds(d * ZP, ZP)
+        return rcopy(
+            zr_out.at[k, :, cut], zr_in.at[k, :, cut], s_zr.at[k, d], r_zr.at[k, d], right
+        )
+
+    def chain_l(k, d):
+        cut = pl.ds(d * ZP, ZP)
+        return rcopy(
+            zl_out.at[k, :, cut], zl_in.at[k, :, cut], s_zl.at[k, d], r_zl.at[k, d], left
+        )
+
+    def z_y(k, d):
+        return rcopy(
+            zy_out.at[k], zy_in.at[k, d - 1], s_zy.at[k, d - 1], r_zy.at[k, d - 1],
+            at(z, ypeer(d), h),
+        )
+
+    def gather_r(k, j, zz):
+        piece = full.at[k, pl.ds(hrow, HV), lanes(zz)]
+        return rcopy(piece, piece, s_ar.at[k, j - 1], r_ar.at[k, j - 1], right)
+
+    def gather_l(k, j, zz):
+        piece = full.at[k, pl.ds(hrow, HV), lanes(zz)]
+        return rcopy(piece, piece, s_al.at[k, j - 1], r_al.at[k, j - 1], left)
 
     def y_ag(k, d):
         piece = full.at[k, frows(y)]
@@ -143,46 +161,164 @@
         )
 
     def flagged(k, start):
-        flag = jnp.full((HV, NP), flag_ref[k], F32).astype(BF)
-        return f_ref[pos_ref[k], pl.ds(start, HV), :] * flag
+        slot = slot_ref[plan_ref[k]]
+        flag = jnp.where(slot // O == col, jnp.float32(1.0), jnp.float32(0.0))
+        return f_ref[slot % O, pl.ds(start, HV), :] * jnp.full((HV, NP), flag, F32).astype(BF)
 
     def st_core(k):
         own[k] = flagged(k, orow)
         core_rs(k).start()
 
-    def st_yrs(k):
+    def st_half(k):
         core_rs(k).wait_recv()
         t1[k] = flagged(k, hrow) + c_in[k]
+
+    def y_send(k):
         for d in range(1, B):
             y_rs(k, d).start()
 
-    def st_zrs(k):
+    def y_sum(k):
         total = t1[k, yrows(y), :]
         for d in range(1, B):
             y_rs(k, d).wait_recv()
             total = total + y_in[k, d - 1]
         t2[k] = total
+
+    def st_sweep_r(k):
+        @pl.when(z == 0)
+        def _():
+            rout[k] = t2[k]
+
+        @pl.when((z > 0) & (z < A - 1))
+        def _():
+            sweep_r(k).wait_recv()
+            rout[k] = t2[k] + rin[k]
+
+        @pl.when(z < A - 1)
+        def _():
+            sweep_r(k).start()
+
+    def st_sweep_l(k):
+        @pl.when(z == A - 1)
+        def _():
+            lout[k] = t2[k]
+
+        @pl.when((z > 0) & (z < A - 1))
+        def _():
+            sweep_l(k).wait_recv()
+            lout[k] = t2[k] + lin[k]
+
+        @pl.when(z > 0)
+        def _():
+            sweep_l(k).start()
+
+    def st_yag(k):
+        @pl.when(z == 0)
+        def _():
+            sweep_l(k).wait_recv()
+            full[k, frows(y), :] = t2[k] + lin[k]
+
+        @pl.when(z == A - 1)
+        def _():
+            sweep_r(k).wait_recv()
+            full[k, frows(y), :] = t2[k] + rin[k]
+
+        @pl.when((z > 0) & (z < A - 1))
+        def _():
+            full[k, frows(y), :] = rout[k] + lin[k]
+
+        for d in range(1, B):
+            y_ag(k, d).start()
+
+    def st_cag(k):
+        for d in range(1, B):
+            y_ag_in(k, d).wait_recv()
+        c_ag(k).start()
+
+    def st_chain_r(k):
         for d in range(1, A):
-            z_rs(k, d).start()
-
-    def st_zag(k):
-        total = t2[k, :, lanes(z)]
-        for d in range(1, A):
-            z_rs(k, d).wait_recv()
-            total = total + z_in[k, d - 1]
-        full[k, frows(y), lanes(z)] = total
-        for d in range(1, A):
-            z_ag(k, d).start()
-
-    def st_yag(k):
-        for d in range(1, A):
-            z_ag_in(k, d).wait_recv()
-        for d in range(1, B):
-            y_ag(k, d).start()
-
-    def st_cag(k):
-        for d in range(1, B):
-            y_ag_in(k, d).wait_recv()
+            cut = slice(d * ZP, (d + 1) * ZP)
+
+            @pl.when((z < d) & (z == 0))
+            def _():
+                zr_out[k, :, cut] = t1[k, :, cut]
+
+            @pl.when((z < d) & (z > 0))
+            def _():
+                chain_r(k, d).wait_recv()
+                zr_out[k, :, cut] = t1[k, :, cut] + zr_in[k, :, cut]
+
+            @pl.when(z < d)
+            def _():
+                chain_r(k, d).start()
+
+    def st_chain_l(k):
+        for d in range(A - 1):
+            cut = slice(d * ZP, (d + 1) * ZP)
+
+            @pl.when((z > d) & (z == A - 1))
+            def _():
+                zl_out[k, :, cut] = t1[k, :, cut]
+
+            @pl.when((z > d) & (z < A - 1))
+            def _():
+                chain_l(k, d).wait_recv()
+                zl_out[k, :, cut] = t1[k, :, cut] + zl_in[k, :, cut]
+
+            @pl.when(z > d)
+            def _():
+                chain_l(k, d).start()
+
+    def st_zy(k):
+        for d in range(A):
+            cut = slice(d * ZP, (d + 1) * ZP)
+
+            @pl.when(z == d)
+            def _():
+                total = t1[k, :, cut]
+                if d > 0:
+                    chain_r(k, d).wait_recv()
+                    total = total + zr_in[k, :, cut]
+                if d < A - 1:
+                    chain_l(k, d).wait_recv()
+                    total = total + zl_in[k, :, cut]
+                zy_out[k] = total
+
+        for d in range(1, B):
+            z_y(k, d).start()
+
+    def st_zysum(k):
+        total = zy_out[k]
+        for d in range(1, B):
+            z_y(k, d).wait_recv()
+            total = total + zy_in[k, d - 1]
+        full[k, pl.ds(hrow, HV), lanes(z)] = total
+
+    def gather_in(k, j):
+        @pl.when(z - j >= 0)
+        def _():
+            gather_r(k, j, lax.rem(z - j + A, A)).wait_recv()
+
+        @pl.when(z + j < A)
+        def _():
+            gather_l(k, j, lax.rem(z + j, A)).wait_recv()
+
+    def gather_out(k, j):
+        @pl.when((z - j + 1 >= 0) & (z < A - 1))
+        def _():
+            gather_r(k, j, lax.rem(z - j + 1 + A, A)).start()
+
+        @pl.when((z + j - 1 < A) & (z > 0))
+        def _():
+            gather_l(k, j, lax.rem(z + j - 1, A)).start()
+
+    def st_gather(j, k):
+        if j > 1:
+            gather_in(k, j - 1)
+        gather_out(k, j)
+
+    def st_zcag(k):
+        gather_in(k, A - 1)
         c_ag(k).start()
 
     def st_comp(k):
@@ -193,8 +329,11 @@
                 source, f_ref[l], (((1,), (1,)), ((), ())), preferred_element_type=F32
             )
             top = 2.0 * ints - jnp.transpose(ints)
-            den = (esrc_ref[k] + eloc_ref[l] - vcol_ref[...]) - vrow_ref[...]
-            wbuf[:, l * V:(l + 1) * V] = (top / den * mask_ref[k * O + l]).astype(BF)
+            den = (occ_ref[plan_ref[k]] + eloc[l][:, :1]) - vsum[...]
+            code = lax.rem(k, SRC) * O + l
+            hits = jnp.where(pairs_ref[pl.ds(k // SRC, 1), :] == code, 1.0, 0.0)
+            listed = jnp.max(hits, axis=1, keepdims=True)
+            wbuf[:, l * V:(l + 1) * V] = (top / den * listed).astype(BF)
         gamma = jnp.dot(
             wbuf[...], f_ref[...].reshape(O * V, NP), preferred_element_type=F32
         )
@@ -224,15 +363,47 @@
             total = total + gz_in[k, d - 1].astype(F32)
         acc[k] = total
 
-    stages = (
-        (D_CORE, st_core), (D_YRS, st_yrs), (D_ZRS, st_zrs), (D_ZAG, st_zag), (D_YAG, st_yag),
-        (D_CAG, st_cag), (D_GEND, st_gend), (D_GZ, st_gz), (D_GY, st_gy), (D_COMP, st_comp),
-    )
+    def z_first(k):
+        return (lax.rem(k, 2) == 1) & (k + 2 < K)
+
+    vrow = jnp.broadcast_to(vrow_ref[...], (V, V))
+    vsum[...] = vrow + jnp.transpose(vrow)
+    for l in range(O):
+        mine = jnp.where(slots_ref[...] == col * O + l, occs_ref[...], 0.0)
+        eloc[l] = jnp.broadcast_to(jnp.sum(mine, axis=1, keepdims=True), (1, 128))
 
     def tick(t, carry):
-        for delay, stage in stages:
+        def run(delay, stage, kind):
             k = t - delay
-            pl.when((k >= 0) & (k < K))(partial(stage, k))
+            kept = (k >= 0) & (k < K)
+            if kind == "z":
+                kept = kept & z_first(k)
+            if kind == "y":
+                kept = kept & jnp.logical_not(z_first(k))
+            pl.when(kept)(partial(stage, k))
+
+        mirror = A - 1 - z
+        run(0, st_core, "")
+        run(1, st_half, "")
+        run(1, y_send, "y")
+        run(1 + z, st_chain_r, "z")
+        run(1 + mirror, st_chain_l, "z")
+        run(2, y_sum, "y")
+        run(2 + z, st_sweep_r, "y")
+        run(2 + mirror, st_sweep_l, "y")
+        run(A, st_zy, "z")
+        run(A + 1, st_yag, "y")
+        run(A + 1, st_zysum, "z")
+        for j in range(1, A):
+            run(A + j, partial(st_gather, j), "z")
+        run(2 * A, st_zcag, "z")
+        run(A + 2, st_cag, "y")
+        y_comp, z_comp = A + 3, 2 * A + 1
+        for comp, kind in ((y_comp, "y"), (z_comp, "z")):
+            run(comp + 3, st_gend, kind)
+            run(comp + 2, st_gz, kind)
+            run(comp + 1, st_gy, kind)
+            run(comp, st_comp, kind)
 
         @pl.when(t == 2)
         def _():
@@ -241,7 +412,7 @@
 
         return carry
 
-    lax.fori_loop(0, K + D_GEND, tick, 0)
+    lax.fori_loop(0, K + 2 * A + 4, tick, 0)
 
     m_local.wait()
     for d in range(1, NR):
@@ -257,15 +428,35 @@
     def drain(k, carry):
         core_rs(k).wait_send()
         for d in range(1, B):
-            y_rs(k, d).wait_send()
-            y_ag(k, d).wait_send()
             g_y(k, d).wait_send()
         for d in range(1, A):
-            z_rs(k, d).wait_send()
-            z_ag(k, d).wait_send()
             g_z(k, d).wait_send()
         c_ag(k).wait_send()
         g_core(k).wait_send()
+
+        @pl.when(jnp.logical_not(z_first(k)))
+        def _():
+            for d in range(1, B):
+                y_rs(k, d).wait_send()
+                y_ag(k, d).wait_send()
+            pl.when(z < A - 1)(lambda: sweep_r(k).wait_send())
+            pl.when(z > 0)(lambda: sweep_l(k).wait_send())
+
+        @pl.when(z_first(k))
+        def _():
+            for d in range(1, B):
+                z_y(k, d).wait_send()
+            for d in range(A):
+                pl.when(z < d)(lambda: chain_r(k, d).wait_send())
+                pl.when(z > d)(lambda: chain_l(k, d).wait_send())
+            for j in range(1, A):
+                pl.when((z - j + 1 >= 0) & (z < A - 1))(
+                    lambda: gather_r(k, j, lax.rem(z - j + 1 + A, A)).wait_send()
+                )
+                pl.when((z + j - 1 < A) & (z > 0))(
+                    lambda: gather_l(k, j, lax.rem(z + j - 1, A)).wait_send()
+                )
+
         return carry
 
     lax.fori_loop(0, K, drain, 0)
@@ -282,35 +473,22 @@
     K = steps * sources
     R = V // n
     HV, YV, ZP = V // 2, V // 2 // B, NP // A
-    column = lax.axis_index("col")
-    occupied = occ_energy.shape[0]
-    local_slots = column * O + jnp.arange(O, dtype=jnp.int32)
-    local_match = orbital_slot[None, :] == local_slots[:, None]
-    local_energy = jnp.sum(jnp.where(local_match, occ_energy[None, :], 0.0), axis=1)
-    plan = source_plan.reshape(K)
-    source_match = plan[:, None] == jnp.arange(occupied, dtype=jnp.int32)[None, :]
-    source_energy = jnp.sum(jnp.where(source_match, occ_energy[None, :], 0.0), axis=1)
-    source_slot = jnp.sum(jnp.where(source_match, orbital_slot[None, :], 0), axis=1)
-    position = (source_slot % O).astype(jnp.int32)
-    flag = (source_slot // O == column).astype(F32)
-    codes = jnp.arange(sources * O, dtype=jnp.int32)
-    pair_mask = jnp.any(
-        pair_list.reshape(steps, -1)[:, :, None] == codes[None, None, :], axis=1
-    ).astype(F32).reshape(K * O)
-
     dma = pltpu.SemaphoreType.DMA
     b1, a1 = max(B - 1, 1), max(A - 1, 1)
     per_k = (K,)
     sems = []
-    for shape in (per_k, (K, b1), (K, a1), (K, a1), (K, b1), per_k, per_k, (K, b1), (K, a1)):
+    for shape in (
+        per_k, (K, b1), per_k, per_k, (K, A), (K, A), (K, b1), (K, a1), (K, a1),
+        (K, b1), per_k, per_k, (K, b1), (K, a1),
+    ):
         sems += [dma(shape), dma(shape)]
     nr1 = max(NR - 1, 1)
     sems += [dma((nr1,)), dma((nr1,)), dma]
     vm = pltpu.VMEM
     out = pl.pallas_call(
-        partial(kernel, (K, A, B, NR, O, V, NP)),
+        partial(kernel, (K, A, B, NR, O, V, NP, sources)),
         out_shape=jax.ShapeDtypeStruct((K, R, NP), F32),
-        in_specs=[pl.BlockSpec(memory_space=pltpu.SMEM)] * 5 + [pl.BlockSpec(memory_space=vm)] * 4,
+        in_specs=[pl.BlockSpec(memory_space=pltpu.SMEM)] * 3 + [pl.BlockSpec(memory_space=vm)] * 6,
         out_specs=pl.BlockSpec(memory_space=vm),
         scratch_shapes=[
             vm((K, HV, NP), BF),
@@ -318,8 +496,19 @@
             vm((K, HV, NP), BF),
             vm((K, b1, YV, NP), BF),
             vm((K, YV, NP), BF),
-            vm((K, a1, YV, ZP), BF),
+            vm((K, YV, NP), BF),
+            vm((K, YV, NP), BF),
+            vm((K, YV, NP), BF),
+            vm((K, YV, NP), BF),
+            vm((K, HV, NP), BF),
+            vm((K, HV, NP), BF),
+            vm((K, HV, NP), BF),
+            vm((K, HV, NP), BF),
+            vm((K, HV, ZP), BF),
+            vm((K, b1, HV, ZP), BF),
             vm((K, V, NP), BF),
+            vm((V, V), F32),
+            vm((O, 1, 128), F32),
             vm((V, O * V), BF),
             vm((K, A, B, 2, R, NP), F32),
             vm((K, A, B, R, NP), BF),
@@ -336,8 +525,9 @@
             collective_id=0, has_side_effects=True, vmem_limit_bytes=60 * 1024 * 1024
         ),
     )(
-        position, flag, source_energy, local_energy, pair_mask,
-        factors, metric_root, vir_energy[:, None], vir_energy[None, :],
+        source_plan.reshape(K), orbital_slot, occ_energy,
+        factors, metric_root, vir_energy[None, :], orbital_slot[None, :], occ_energy[None, :],
+        pair_list.reshape(steps, -1),
     )
     return jnp.transpose(out, (1, 0, 2))[None]
 

time: 109 us -> 100 us (0.917)
  other arithmetic: 5.54 us -> 0 us
  local copies, waits for them, and re-layouts: 4.96 us -> 3.41 us
  Pallas kernels: 97.9 us -> 96.4 us
    reduce_sum x3 -> x0, other arithmetic: 3.65 us -> none  [the longest x1 1.42 us: on_device(): jnp.sum(jnp.where(source_match, occ_energy[None, :], 0.0), axis=1)]
    broadcast_in_dim x1 -> x0, local copies, waits for them, and re-layouts: 1.47 us -> none  [on_device(): vir_energy[:, None]]
    pallas_call x1, Pallas kernels: 97.9 us -> 96.4 us  [on_device(): pl.pallas_call(partial(kernel, (K, A, B, NR, O, V, NP, sources)), out_sha...]
    reshape x0 -> x1, local copies, waits for them, and re-layouts: none -> 1.27 us  [on_device(): source_plan.reshape(K)]
where the time goes in v2:
time: 100 us; the launch traced here: 99.8 us
  Pallas kernels  96.4 us (96%)
  local copies, waits for them, and re-layouts  3.41 us (3%)
    pallas_call x1, Pallas kernels, on_device(): pl.pallas_call(partial(kernel, (K, A, B, NR, O, V, NP, sources)), out_sha...  96.4 us
    broadcast_in_dim x1, local copies, waits for them, and re-layouts, on_device(): return jnp.transpose(out, (1, 0, 2))[None]  2.14 us

profile of v2, /device:TPU:0, one launch (start us, length us, event | category | flops | bytes accessed | tf_op | source)
XLA Modules:
  0.0 99.8 jit_solution(3211370050107954581)
XLA Ops:
  0.0 1.3 %reshape.6.plan_ref = s32[8]{0:T(128)} reshape(s32[1,2,4]{2,1,0:T(2,128)} %param.12) | data formatting | bytes 64 | tf_op jit(solution)/shard_map/reshape | solution.py:528
  1.3 96.4 %shard_map.73 = f32[8,16,1024]{2,1,0:T(8,128)} custom-call(s32[8]{0:T(128)} %reshape.6.plan_ref, s32[96]{0:T(128)} %slot_ref.1, f32[96]{0:T(128)} %occ_ref.1, bf16[6,256,1024]{2,1,0:T(8,128)(2,1)} %f_ref.1, bf16[512,1024]{1,0:T(8,128)(2,1)} %metric_ref.1, f32[1,256]{1,0:T(1,128)} %bitcast.10, s32[1,96]{1,0:T(1,128)} %bitcast.8, f32[1,96]{1,0:T(1,128)} %bitcast.9, ...), custom_call_target="tpu_custom_call" | custom-call | tf_op jit(solution)/shard_map/pallas_call | solution.py:488
  97.7 2.1 %copy.8 = f32[1,16,8,1024]{3,2,1,0:T(8,128)} copy(f32[1,16,8,1024]{3,1,2,0:T(8,128)} %bitcast.7) | data formatting | bytes 1048576 | tf_op jit(solution)/shard_map/broadcast_in_dim | solution.py:532

commit v3 on v2

--- a/solution.py
+++ b/solution.py
@@ -364,7 +364,7 @@
         acc[k] = total
 
     def z_first(k):
-        return (lax.rem(k, 2) == 1) & (k + 2 < K)
+        return (lax.rem(k, 2) == 0) & (2 * k < K)
 
     vrow = jnp.broadcast_to(vrow_ref[...], (V, V))
     vsum[...] = vrow + jnp.transpose(vrow)

time: 100 us -> 97.2 us (0.972)
  Pallas kernels: 96.4 us -> 93.6 us
    pallas_call x1, Pallas kernels: 96.4 us -> 93.6 us  [on_device(): pl.pallas_call(partial(kernel, (K, A, B, NR, O, V, NP, sources)), out_sha...]
where the time goes in v3:
time: 97.2 us; the launch traced here: 97 us
  Pallas kernels  93.6 us (96%)
  local copies, waits for them, and re-layouts  3.41 us (4%)
    pallas_call x1, Pallas kernels, on_device(): pl.pallas_call(partial(kernel, (K, A, B, NR, O, V, NP, sources)), out_sha...  93.6 us
    broadcast_in_dim x1, local copies, waits for them, and re-layouts, on_device(): return jnp.transpose(out, (1, 0, 2))[None]  2.14 us

profile of v3, /device:TPU:0, one launch (start us, length us, event | category | flops | bytes accessed | tf_op | source)
XLA Modules:
  0.0 97.0 jit_solution(17039796466336084275)
XLA Ops:
  0.0 1.3 %reshape.6.plan_ref = s32[8]{0:T(128)} reshape(s32[1,2,4]{2,1,0:T(2,128)} %param.12) | data formatting | bytes 64 | tf_op jit(solution)/shard_map/reshape | solution.py:528
  1.3 93.6 %shard_map.73 = f32[8,16,1024]{2,1,0:T(8,128)} custom-call(s32[8]{0:T(128)} %reshape.6.plan_ref, s32[96]{0:T(128)} %slot_ref.1, f32[96]{0:T(128)} %occ_ref.1, bf16[6,256,1024]{2,1,0:T(8,128)(2,1)} %f_ref.1, bf16[512,1024]{1,0:T(8,128)(2,1)} %metric_ref.1, f32[1,256]{1,0:T(1,128)} %bitcast.10, s32[1,96]{1,0:T(1,128)} %bitcast.8, f32[1,96]{1,0:T(1,128)} %bitcast.9, ...), custom_call_target="tpu_custom_call" | custom-call | tf_op jit(solution)/shard_map/pallas_call | solution.py:488
  94.9 2.1 %copy.8 = f32[1,16,8,1024]{3,2,1,0:T(8,128)} copy(f32[1,16,8,1024]{3,1,2,0:T(8,128)} %bitcast.7) | data formatting | bytes 1048576 | tf_op jit(solution)/shard_map/broadcast_in_dim | solution.py:532
